TPU v7x, 32 devices: a whole 2x2x4 slice. The times are simulated.
32 devices in a mesh: peer: 8 (over z, y), grp: 4 (over x, core).
Axes of the slice: x: 2, y: 2, z: 4, core: 2. Of those that a mesh axis runs over, the one named last changes fastest.
Arguments:
- tokens: bfloat16 [4096, 2048], P(('peer', 'grp')), may hold values from -6 to 6
- cotangent: bfloat16 [4096, 2048], P(('peer', 'grp')), may hold values from -6 to 6
- expert_ids: int32 [4096, 4], P(('peer', 'grp')), may hold values from 0 to 31, all different within a row; in each aligned block of 128 rows (0 to 127, 128 to 255, ...) at most 32 rows name the same one
- route_prob: float32 [4096, 4], P(('peer', 'grp')), may hold values from 0.1 to 1
- w_gate: bfloat16 [8, 2048, 704], P('peer', None, 'grp'), may hold values from -0.125 to 0.125
- w_up: bfloat16 [8, 2048, 704], P('peer', None, 'grp'), may hold values from -0.125 to 0.125
- w_down: bfloat16 [8, 704, 2048], P('peer', 'grp'), may hold values from -0.21875 to 0.21875
- student_logits: bfloat16 [8, 8, 151936], P('peer', None, 'grp'), may hold values from -24 to 252
- stale_logits: bfloat16 [8, 8, 151936], P('peer', None, 'grp'), may hold values from -24 to 252
- labels: int32 [8, 8], P('peer'), may hold values from 0 to 151935
Outputs:
- layer_out: bfloat16 [4096, 2048], P(('peer', 'grp'))
- input_grad: bfloat16 [4096, 2048], P(('peer', 'grp'))
- prob_grad: float32 [4096, 4], P(('peer', 'grp'))
- distill_loss: float32 [8, 8], P('peer')
- logit_grad: bfloat16 [8, 8, 151936], P('peer', None, 'grp')
Inputs may be any that keep to these rules, and one draw needn't show every extreme that they name: `expert_ids`: each row names 4 different experts; the rows of one device name any one expert at most 32 times.
All inputs are finite; a program needn't handle non-finite values.
Results may differ from a plain program's by a relative error of at most 0.0064.
Values may be sent and summed in bfloat16 or wider, within the bound.
No kernel may reach another device: no remote copies, remote signals or barrier semaphores. Data moves between devices by JAX's collectives and lax.ppermute only.
A program may use at most 64 MiB of HBM per device.

v0:
```python
import jax
import jax.numpy as jnp
from jax import lax
from jax.sharding import PartitionSpec as P

PIECES = 4
CAP = 32


def joined(value, axis, combine):
    everything = jax.tree.map(lambda part: lax.all_gather(part, axis), value)
    leading = jax.tree.map(lambda part: part[0], everything)

    def lap(k, so_far):
        return combine(so_far, jax.tree.map(lambda part: part[k], everything))

    return lax.fori_loop(1, lax.axis_size(axis), lap, leading)


def from_behind(value, axis, steps):
    count = lax.axis_size(axis)
    pairs = [(source, (source + steps) % count) for source in range(count)]
    return lax.ppermute(value, axis, pairs)


def slot_tables(expert_ids, n_window, capacity):
    window_iota = lax.broadcasted_iota(jnp.int32, (1, 1, n_window), 2)
    member = jnp.sum((expert_ids[:, :, None] == window_iota).astype(jnp.int32), axis=1)
    position = jnp.cumsum(member, axis=0) - member
    slot_iota = lax.broadcasted_iota(jnp.int32, (1, capacity, 1), 1)
    select = (position.T[:, None, :] == slot_iota) & (member.T[:, None, :] > 0)
    return (position, select)


def forward_piece(slot_rows, gate_cols, up_cols, down_rows):
    gate_act = jnp.dot(slot_rows, gate_cols, preferred_element_type=jnp.float32)
    up_act = jnp.dot(slot_rows, up_cols, preferred_element_type=jnp.float32)
    hidden = (gate_act * jax.nn.sigmoid(gate_act) * up_act).astype(jnp.bfloat16)
    piece_out = jnp.dot(hidden, down_rows, preferred_element_type=jnp.float32).astype(jnp.bfloat16)
    return (piece_out, gate_act, up_act)


def backward_piece(scaled_rows, gate_act, up_act, gate_cols, up_cols, down_rows):
    contract = (((1,), (1,)), ((), ()))
    grad_hidden = lax.dot_general(
        scaled_rows, down_rows, contract, preferred_element_type=jnp.float32
    )
    sigmoid_gate = jax.nn.sigmoid(gate_act)
    grad_gate = (
        grad_hidden * up_act * sigmoid_gate * (1.0 + gate_act * (1.0 - sigmoid_gate))
    ).astype(jnp.bfloat16)
    grad_up = (grad_hidden * gate_act * sigmoid_gate).astype(jnp.bfloat16)
    piece_grad = lax.dot_general(grad_gate, gate_cols, contract, preferred_element_type=jnp.float32)
    piece_grad = piece_grad + lax.dot_general(
        grad_up, up_cols, contract, preferred_element_type=jnp.float32
    )
    return piece_grad.astype(jnp.bfloat16)


def join_stats(first_side, second_side):
    max_one, sum_one, tmax_one, tsum_one, cross_one, label_one = first_side
    max_two, sum_two, tmax_two, tsum_two, cross_two, label_two = second_side
    max_both = jnp.maximum(max_one, max_two)
    tmax_both = jnp.maximum(tmax_one, tmax_two)
    scale_one = jnp.exp(tmax_one - tmax_both)
    scale_two = jnp.exp(tmax_two - tmax_both)
    sum_both = sum_one * jnp.exp(max_one - max_both) + sum_two * jnp.exp(max_two - max_both)
    tsum_both = tsum_one * scale_one + tsum_two * scale_two
    cross_both = cross_one * scale_one + cross_two * scale_two
    return (max_both, sum_both, tmax_both, tsum_both, cross_both, label_one + label_two)


def distill(student_logits, teacher_now, labels):
    student = student_logits[0].astype(jnp.float32)
    teacher = teacher_now[0].astype(jnp.float32)
    shard_width = student.shape[1]
    vocab_ids = lax.axis_index("grp") * shard_width + lax.broadcasted_iota(
        jnp.int32, student.shape, 1
    )
    label_hit = vocab_ids == labels[0][:, None]
    label_logit = jnp.sum(jnp.where(label_hit, student, 0.0), axis=1)
    local_smax = jnp.max(student, axis=1)
    local_tmax = jnp.max(teacher, axis=1)
    student_exp = jnp.sum(jnp.exp(student - local_smax[:, None]), axis=1)
    teacher_exp = jnp.exp(teacher - local_tmax[:, None])
    teacher_sum = jnp.sum(teacher_exp, axis=1)
    cross_sum = jnp.sum(teacher_exp * (teacher - student), axis=1)
    max_student, student_sum, max_teacher, teacher_sum, cross_sum, label_logit = joined(
        (local_smax, student_exp, local_tmax, teacher_sum, cross_sum, label_logit),
        "grp",
        join_stats,
    )
    lse_student = max_student + jnp.log(student_sum)
    lse_teacher = max_teacher + jnp.log(teacher_sum)
    distill_loss = 2.0 * lse_student - label_logit + cross_sum / teacher_sum - lse_teacher
    teacher_prob = jnp.exp(teacher - lse_teacher[:, None])
    logit_grad = (
        2.0 * jnp.exp(student - lse_student[:, None]) - label_hit.astype(jnp.float32) - teacher_prob
    ).astype(jnp.bfloat16)
    return (distill_loss[None], logit_grad[None])


def body(
    tokens,
    cotangent,
    expert_ids,
    route_prob,
    w_gate,
    w_up,
    w_down,
    student_logits,
    stale_logits,
    labels,
):
    group_size = lax.axis_size("grp")
    n_window = group_size // PIECES
    gate_cols = w_gate[0]
    up_cols = w_up[0]
    down_rows = w_down[0]
    model_width = tokens.shape[1]
    half_cap = CAP // 2
    position, select = slot_tables(expert_ids, n_window, CAP)
    select_bf = select.astype(jnp.bfloat16)
    window_iota = lax.broadcasted_iota(jnp.int32, (1, 1, n_window), 2)
    token_prob = jnp.sum(
        route_prob[:, :, None] * (expert_ids[:, :, None] == window_iota).astype(jnp.float32), axis=1
    )
    slot_prob = jnp.einsum(
        "ect,te->ec", select.astype(jnp.float32), token_prob, precision=lax.Precision.HIGHEST
    )
    slot_rows = jnp.einsum(
        "ect,td->ecd", select_bf, tokens, preferred_element_type=jnp.float32
    ).astype(jnp.bfloat16)
    slot_cot = jnp.einsum("ect,td->ecd", select_bf, cotangent, preferred_element_type=jnp.float32)
    slot_scaled = (slot_prob[:, :, None] * slot_cot).astype(jnp.bfloat16)
    send_rows = jnp.repeat(slot_rows, PIECES, axis=0).reshape(group_size, 2, half_cap, model_width)
    send_scaled = jnp.repeat(slot_scaled, PIECES, axis=0).reshape(
        group_size, 2, half_cap, model_width
    )
    recv_rows = lax.all_to_all(send_rows, "grp", split_axis=0, concat_axis=0, tiled=True)
    recv_scaled = lax.all_to_all(send_scaled, "grp", split_axis=0, concat_axis=0, tiled=True)
    item_count = recv_rows.shape[1]
    flat_rows = recv_rows.reshape(-1, model_width)
    flat_scaled = recv_scaled.reshape(-1, model_width)
    piece_out, gate_act, up_act = forward_piece(flat_rows, gate_cols, up_cols, down_rows)
    piece_out = piece_out.reshape(group_size, item_count, half_cap, model_width)
    piece_grad = backward_piece(flat_scaled, gate_act, up_act, gate_cols, up_cols, down_rows)
    piece_grad = piece_grad.reshape(group_size, item_count, half_cap, model_width)
    back_out = lax.all_to_all(piece_out, "grp", split_axis=0, concat_axis=0, tiled=True)
    back_grad = lax.all_to_all(piece_grad, "grp", split_axis=0, concat_axis=0, tiled=True)
    back_out, back_grad = (back_out, back_grad)
    expert_out = jnp.sum(
        back_out.astype(jnp.float32).reshape(n_window, PIECES, CAP, model_width), axis=1
    )
    expert_grad = jnp.sum(
        back_grad.astype(jnp.float32).reshape(n_window, PIECES, CAP, model_width), axis=1
    )
    in_window = expert_ids < n_window
    safe_ids = jnp.where(in_window, expert_ids, 0)
    slot_index = jnp.take_along_axis(position, safe_ids, axis=1)
    flat_index = safe_ids * CAP + slot_index
    out_rows = jnp.where(
        in_window[:, :, None],
        jnp.take(expert_out.reshape(-1, model_width), flat_index, axis=0),
        0.0,
    )
    grad_rows = jnp.where(
        in_window[:, :, None],
        jnp.take(expert_grad.reshape(-1, model_width), flat_index, axis=0),
        0.0,
    )
    layer_out = jnp.sum(route_prob[:, :, None] * out_rows, axis=1).astype(jnp.bfloat16)
    prob_grad = jnp.sum(cotangent.astype(jnp.float32)[:, None, :] * out_rows, axis=2)
    input_grad = jnp.sum(grad_rows, axis=1).astype(jnp.bfloat16)
    teacher_now = from_behind(stale_logits, "peer", 1)
    distill_loss, logit_grad = distill(student_logits, teacher_now, labels)
    return (layer_out, input_grad, prob_grad, distill_loss, logit_grad)


def solution(mesh):
    placed = (
        P(("peer", "grp"), None),
        P(("peer", "grp"), None),
        P(("peer", "grp"), None),
        P(("peer", "grp"), None),
        P("peer", None, "grp"),
        P("peer", None, "grp"),
        P("peer", "grp", None),
        P("peer", None, "grp"),
        P("peer", None, "grp"),
        P("peer", None),
    )
    return jax.shard_map(
        body,
        mesh=mesh,
        in_specs=placed,
        out_specs=(
            P(("peer", "grp"), None),
            P(("peer", "grp"), None),
            P(("peer", "grp"), None),
            P("peer", None),
            P("peer", None, "grp"),
        ),
        check_vma=False,
    )
```

profile of v0, /device:TPU:0, one launch (start us, length us, event | category | flops | bytes accessed | tf_op | source)
XLA Modules:
  0.0 88.1 jit_solution(13793682521302028346)
XLA Ops:
  0.6 3.0 %collective-permute-start = (bf16[1,8,37984]{2,1,0:T(8,128)(2,1)}, bf16[1,8,37984]{2,1,0:T(8,128)(2,1)S(1)}, u32[]{:S(2)}, u32[]{:S(2)}) collective-permute-start(bf16[1,8,37984]{2,1,0:T(8,128)(2,1)} %param.22), channel_id=1, source_target_pairs={{0,4},{4,8},{8,12},{12,16},{16,20},{20,24},{24,28},{28,0},{1,5},{5... | collective-permute-start | bytes 1823240 | tf_op jit(solution)/shard_map/ppermute | solution.py:23
  3.7 0.7 select_reduce_fusion
  4.4 0.1 copy.42
  4.6 0.2 reduce_window_sum.13
  4.9 1.2 %convolution_convert_fusion.1 = bf16[32,2048]{1,0:T(8,128)(2,1)S(1)} fusion(bf16[128,2048]{1,0:T(8,128)(2,1)} %param.14, s32[128]{0:T(128)S(1)} %sub.111, pred[128]{0:T(512)(128)(4,1)S(1)} %broadcast_compare_fusion.2), kind=kOutput, calls=%fused_computation.36 | convolution fusion | flops 16850944 | bytes 656000 | tf_op jit(solution)/shard_map/ect,td->ecd/dot_general | solution.py:131
  6.1 0.8 broadcast_in_dim.63
  7.0 3.5 %all-to-all-start = ((bf16[4,2,16,2048]{3,2,1,0:T(8,128)(2,1)}), bf16[4,2,16,2048]{3,2,1,0:T(8,128)(2,1)S(1)}, u32[]{:S(2)}, u32[]{:S(2)}) async-start(bf16[4,2,16,2048]{3,2,1,0:T(8,128)(2,1)} %broadcast_in_dim.63), calls=%async_computation | async-start | bytes 1048576 | tf_op jit(solution)/shard_map/all_to_all | solution.py:140
  10.5 0.1 copy.44
  10.6 0.1 reshape.285
  10.8 3.4 %gather_fusion = s32[512]{0:T(512)S(1)} fusion(s32[128,1]{1,0:T(8,128)S(1)} %get-tuple-element.386, s32[512]{0:T(512)S(1)} %reshape.285), kind=kCustom, calls=%fused_computation.2 | custom fusion | bytes 8192 | tf_op jit(solution)/shard_map/jit(take_along_axis)/gather | solution.py:160
  14.4 0.1 copy.47
  14.5 0.1 reshape.348
  14.6 0.4 reduce_max.36
  15.1 0.6 dynamic-slice
  16.4 0.7 copy.40
  17.2 0.1 copy.41
  17.3 0.1 copy.46
  17.5 1.2 %convert_element_type.89 = f32[128,2048]{1,0:T(8,128)} convert(bf16[128,2048]{1,0:T(8,128)(2,1)S(1)} %copy-done.5) | non-fusion elementwise | flops 262144 | bytes 1572864 | tf_op jit(solution)/shard_map/convert_element_type | solution.py:173
  18.6 0.1 convolution_bitcast_fusion
  18.7 0.2 fusion.17
  19.0 0.2 all-to-all-done
  19.2 0.8 broadcast_in_dim.67
  20.1 4.3 %all-to-all-start.2 = ((bf16[4,2,16,2048]{3,2,1,0:T(8,128)(2,1)}), bf16[4,2,16,2048]{3,2,1,0:T(8,128)(2,1)}, u32[]{:S(2)}, u32[]{:S(2)}) async-start(bf16[4,2,16,2048]{3,2,1,0:T(8,128)(2,1)} %broadcast_in_dim.67), calls=%async_computation.2 | async-start | bytes 1048576 | tf_op jit(solution)/shard_map/all_to_all | solution.py:141
  24.3 0.4 fusion.43
  24.7 1.0 %fusion.39 = f32[128,176]{0,1:T(8,128)} fusion(bf16[128,2048]{1,0:T(8,128)(2,1)S(1)} %bitcast.127, bf16[1,2048,176]{1,2,0:T(8,128)(2,1)S(1)} %copy-done.3), kind=kOutput, calls=%fused_computation.65 | convolution fusion | flops 92274688 | bytes 1335296 | tf_op jit(solution)/shard_map/dot_general | solution.py:37
  25.8 7.4 %all-to-all-done.2 = bf16[4,2,16,2048]{3,2,1,0:T(8,128)(2,1)} async-done(((bf16[4,2,16,2048]{3,2,1,0:T(8,128)(2,1)}), bf16[4,2,16,2048]{3,2,1,0:T(8,128)(2,1)}, u32[]{:S(2)}, u32[]{:S(2)}) %all-to-all-start.2) | async-done | bytes 524320 | tf_op jit(solution)/shard_map/all_to_all | solution.py:141
  33.2 1.6 %fusion.35 = f32[128,176]{0,1:T(8,128)S(1)} fusion(bf16[128,2048]{1,0:T(8,128)(2,1)} %bitcast.18, bf16[1,176,2048]{2,1,0:T(8,128)(2,1)} %param.20), kind=kOutput, calls=%fused_computation.61 | convolution fusion | flops 92274688 | bytes 1335296 | tf_op jit(solution)/shard_map/dot_general | solution.py:45
  34.8 0.4 fusion.41
  35.2 1.1 %fusion.16 = bf16[128,2048]{1,0:T(8,128)(2,1)} fusion(f32[128,2048]{1,0:T(8,128)S(1)} %fusion.41, bf16[1,2048,176]{1,2,0:T(8,128)(2,1)S(1)} %copy-done.3, f32[128,176]{0,1:T(8,128)S(1)} %fusion.35, f32[128,176]{0,1:T(8,128)S(1)} %fusion.43), kind=kOutput, calls=%fused_computation.32 | convolution fusion | flops 92934144 | bytes 2473984 | tf_op jit(solution)/shard_map/dot_general | solution.py:54
  36.4 3.6 %all-to-all-start.3 = ((bf16[4,2,16,2048]{3,2,1,0:T(8,128)(2,1)}), bf16[4,2,16,2048]{3,2,1,0:T(8,128)(2,1)S(1)}, u32[]{:S(2)}, u32[]{:S(2)}) async-start(bf16[4,2,16,2048]{3,2,1,0:T(8,128)(2,1)} %bitcast.19), calls=%async_computation.3 | async-start | bytes 1048576 | tf_op jit(solution)/shard_map/all_to_all | solution.py:150
  40.0 2.0 %convolution_convert_fusion = bf16[128,2048]{1,0:T(8,128)(2,1)} fusion(bf16[1,176,2048]{2,1,0:T(8,128)(2,1)S(1)} %copy-done.4, f32[128,176]{0,1:T(8,128)} %fusion.39, f32[128,176]{0,1:T(8,128)S(1)} %fusion.43), kind=kOutput, calls=%fused_computation.33 | convolution fusion | flops 92672000 | bytes 1425408 | tf_op jit(solution)/shard_map/dot_general | solution.py:39
  42.0 0.4 reduce_max.40
  42.6 1.2 %fusion.33 = (f32[8]{0:T(128)S(1)}, f32[8]{0:T(128)S(1)}, f32[8]{0:T(128)S(1)}, f32[8]{0:T(128)S(1)}) fusion(bf16[1,8,37984]{2,1,0:T(8,128)(2,1)S(1)} %collective-permute-done, bf16[1,8,37984]{2,1,0:T(8,128)(2,1)S(1)} %copy-done.1, f32[8]{0:T(128)S(1)} %reduce_max.45, s32[8]{0:T(128)S(1)} %bitcast.137, s32[37984]{0:T(1024)S(1)} %iota_add_fusion, ...), kind=kLoop, calls=%fused_computation.56 | loop fusion | flops 3646432 | bytes 1367648 | tf_op jit(solution)/shard_map/reduce_sum | solution.py:87
  43.7 0.2 dynamic-update-slice.1
  44.0 0.2 dynamic-update-slice.3
  44.2 0.2 dynamic-update-slice.4
  44.4 0.2 dynamic-update-slice.5
  44.6 7.3 %all-reduce.6 = (f32[32]{0:T(128)S(1)}, f32[32]{0:T(128)S(1)}, f32[32]{0:T(128)S(1)}, f32[32]{0:T(128)S(1)}, f32[32]{0:T(128)S(1)}, /*index=5*/f32[32]{0:T(128)S(1)}) all-reduce(f32[32]{0:T(128)S(1)} %convert_dynamic-update-slice_fusion.1, f32[32]{0:T(128)S(1)} %dynamic-update-slice.1, ...), channel_id=2, replica_groups=mesh['peer'=8,'grp'=4] {'grp'}, use_global_device_ids=true, to_apply=%add | all-reduce | flops 192 | bytes 1536
  52.4 0.3 while.25
  52.7 0.5 subtract_bitcast_fusion
  53.2 3.7 %all-to-all-start.1 = ((bf16[4,2,16,2048]{3,2,1,0:T(8,128)(2,1)}), bf16[4,2,16,2048]{3,2,1,0:T(8,128)(2,1)S(1)}, u32[]{:S(2)}, u32[]{:S(2)}) async-start(bf16[4,2,16,2048]{3,2,1,0:T(8,128)(2,1)} %bitcast.128), calls=%async_computation.1 | async-start | bytes 1048576 | tf_op jit(solution)/shard_map/all_to_all | solution.py:149
  56.9 1.4 %fusion.29 = bf16[1,8,37984]{2,1,0:T(8,128)(2,1)} fusion(bf16[1,8,37984]{2,1,0:T(8,128)(2,1)S(1)} %copy-done.1, bf16[1,8,37984]{2,1,0:T(8,128)(2,1)S(1)} %collective-permute-done, f32[8]{0:T(128)S(1)} %get-tuple-element.380, s32[37984]{0:T(1024)S(1)} %iota_add_fusion, f32[8]{0:T(128)S(1)} %get-tuple-element.379, s32[8]{0:T(128)S(1)} %bitcast.138), kind=kLoop, calls=%fused_computation.52 | loop fusion | flops 3038720 | bytes 1975264 | tf_op jit(solution)/shard_map/convert_element_type | solution.py:99
  58.4 3.6 %gather_fusion.2 = f32[512,2048]{1,0:T(8,128)} fusion(f32[32,2048]{1,0:T(8,128)S(1)} %bitcast.125, s32[1024]{0:T(1024)S(1)} %pad_clamp_fusion), kind=kCustom, calls=%fused_computation.1.clone | custom fusion | bytes 8390656 | tf_op jit(solution)/shard_map/jit(_take)/gather | solution.py:169
  62.0 5.2 %reshape.355 = f32[128,4,2048]{2,1,0:T(4,128)} reshape(f32[512,2048]{1,0:T(8,128)} %gather_fusion.2) | data formatting | bytes 8388608 | tf_op jit(solution)/shard_map/jit(_take)/gather | solution.py:169
  67.3 3.6 %gather_fusion.1 = f32[512,2048]{1,0:T(8,128)} fusion(f32[32,2048]{1,0:T(8,128)S(1)} %bitcast.124, s32[1024]{0:T(1024)S(1)} %pad_clamp_fusion), kind=kCustom, calls=%fused_computation.clone | custom fusion | bytes 8390656 | tf_op jit(solution)/shard_map/jit(_take)/gather | solution.py:164
  70.9 5.3 %reshape.351 = f32[128,4,2048]{2,1,0:T(4,128)} reshape(f32[512,2048]{1,0:T(8,128)} %gather_fusion.1) | data formatting | bytes 8388608 | tf_op jit(solution)/shard_map/jit(_take)/gather | solution.py:164
  76.1 11.4 %multiply_reduce_fusion = (f32[128,4]{1,0:T(8,128)S(1)}, bf16[128,2048]{1,0:T(8,128)(2,1)}, bf16[128,2048]{1,0:T(8,128)(2,1)}) fusion(f32[128,4,2048]{2,1,0:T(4,128)} %reshape.351, f32[128,2048]{1,0:T(8,128)S(1)} %copy-done.2, pred[128,4]{1,0:T(8,128)(4,1)S(1)} %copy.46, pred[128,4]{1,0:T(8,128)(4,1)S(1)} %copy.41, f32[128,4]{1,0:T(8,128)S(1)} %copy-done.7, ...), kind=kLoop, calls=%fused_computation.29 | loop fusion | flops 8912384 | bytes 10490880 | tf_op jit(solution)/shard_map/reduce_sum | solution.py:173
  87.5 0.7 copy.50
  (67 shorter events, 1.5 us)
Async XLA Ops:
  0.6 23.7 %copy-start = (bf16[1,2048,176]{1,2,0:T(8,128)(2,1)S(1)}, bf16[1,2048,176]{1,2,0:T(8,128)(2,1)}, u32[]{:S(2)}) copy-start(bf16[1,2048,176]{1,2,0:T(8,128)(2,1)} %param.18) | copy-start | bytes 2162692
  0.6 41.4 %collective-permute-start = (bf16[1,8,37984]{2,1,0:T(8,128)(2,1)}, bf16[1,8,37984]{2,1,0:T(8,128)(2,1)S(1)}, u32[]{:S(2)}, u32[]{:S(2)}) collective-permute-start(bf16[1,8,37984]{2,1,0:T(8,128)(2,1)} %param.22), channel_id=1, source_target_pairs={{0,4},{4,8},{8,12},{12,16},{16,20},{20,24},{24,28},{28,0},{1,5},{5... | collective-permute-start | bytes 1823240 | tf_op jit(solution)/shard_map/ppermute | solution.py:23
  4.8 5.6 %copy-start.8 = (s32[128,4]{0,1:T(4,128)S(1)}, s32[128,4]{0,1:T(4,128)}, u32[]{:S(2)}) copy-start(s32[128,4]{0,1:T(4,128)} %param.16) | copy-start | bytes 6148
  7.0 12.3 %all-to-all-start = ((bf16[4,2,16,2048]{3,2,1,0:T(8,128)(2,1)}), bf16[4,2,16,2048]{3,2,1,0:T(8,128)(2,1)S(1)}, u32[]{:S(2)}, u32[]{:S(2)}) async-start(bf16[4,2,16,2048]{3,2,1,0:T(8,128)(2,1)} %broadcast_in_dim.63), calls=%async_computation | async-start | bytes 1048576 | tf_op jit(solution)/shard_map/all_to_all | solution.py:140
  10.7 3.9 %copy-start.1 = (bf16[1,8,37984]{2,1,0:T(8,128)(2,1)S(1)}, bf16[1,8,37984]{2,1,0:T(8,128)(2,1)}, u32[]{:S(2)}) copy-start(bf16[1,8,37984]{2,1,0:T(8,128)(2,1)} %param.21) | copy-start | bytes 1823236
  10.7 4.3 %copy-start.11 = (u32[32]{0:T(128)S(1)}, u32[32]{0:T(128)}, u32[]{:S(2)}) copy-start(u32[32]{0:T(128)} %constant.107) | copy-start | bytes 388
  10.7 5.7 %copy-start.9 = (f32[128,4]{0,1:T(4,128)S(1)}, f32[128,4]{0,1:T(4,128)}, u32[]{:S(2)}) copy-start(f32[128,4]{0,1:T(4,128)} %param.17) | copy-start | bytes 6148
  14.2 3.3 %copy-start.5 = (bf16[128,2048]{1,0:T(8,128)(2,1)S(1)}, bf16[128,2048]{1,0:T(8,128)(2,1)}, u32[]{:S(2)}) copy-start(bf16[128,2048]{1,0:T(8,128)(2,1)} %param.15) | copy-start | bytes 1572868
  20.1 4.7 %copy-start.3 = (bf16[1,2048,176]{1,2,0:T(8,128)(2,1)S(1)}, bf16[1,2048,176]{1,2,0:T(8,128)(2,1)}, u32[]{:S(2)}) copy-start(bf16[1,2048,176]{1,2,0:T(8,128)(2,1)} %param.19) | copy-start | bytes 2162692
  20.1 13.1 %all-to-all-start.2 = ((bf16[4,2,16,2048]{3,2,1,0:T(8,128)(2,1)}), bf16[4,2,16,2048]{3,2,1,0:T(8,128)(2,1)}, u32[]{:S(2)}, u32[]{:S(2)}) async-start(bf16[4,2,16,2048]{3,2,1,0:T(8,128)(2,1)} %broadcast_in_dim.67), calls=%async_computation.2 | async-start | bytes 1048576 | tf_op jit(solution)/shard_map/all_to_all | solution.py:141
  25.8 9.1 %copy-start.6 = (f32[128,176]{0,1:T(8,128)S(1)}, f32[128,176]{0,1:T(8,128)}, u32[]{:S(2)}) copy-start(f32[128,176]{0,1:T(8,128)} %fusion.39) | copy-start | bytes 270340
  36.4 3.6 %copy-start.4 = (bf16[1,176,2048]{2,1,0:T(8,128)(2,1)S(1)}, bf16[1,176,2048]{2,1,0:T(8,128)(2,1)}, u32[]{:S(2)}) copy-start(bf16[1,176,2048]{2,1,0:T(8,128)(2,1)} %param.20) | copy-start | bytes 2162692
  36.4 16.9 %all-to-all-start.3 = ((bf16[4,2,16,2048]{3,2,1,0:T(8,128)(2,1)}), bf16[4,2,16,2048]{3,2,1,0:T(8,128)(2,1)S(1)}, u32[]{:S(2)}, u32[]{:S(2)}) async-start(bf16[4,2,16,2048]{3,2,1,0:T(8,128)(2,1)} %bitcast.19), calls=%async_computation.3 | async-start | bytes 1048576 | tf_op jit(solution)/shard_map/all_to_all | solution.py:150
  40.0 2.6 %copy-start.10 = (s32[1,8]{1,0:T(1,128)S(1)}, s32[1,8]{1,0:T(1,128)}, u32[]{:S(2)}) copy-start(s32[1,8]{1,0:T(1,128)} %param.23) | copy-start | bytes 100
  53.2 14.0 %all-to-all-start.1 = ((bf16[4,2,16,2048]{3,2,1,0:T(8,128)(2,1)}), bf16[4,2,16,2048]{3,2,1,0:T(8,128)(2,1)S(1)}, u32[]{:S(2)}, u32[]{:S(2)}) async-start(bf16[4,2,16,2048]{3,2,1,0:T(8,128)(2,1)} %bitcast.128), calls=%async_computation.1 | async-start | bytes 1048576 | tf_op jit(solution)/shard_map/all_to_all | solution.py:149
  70.9 5.3 %copy-start.2 = (f32[128,2048]{1,0:T(8,128)S(1)}, f32[128,2048]{1,0:T(8,128)}, u32[]{:S(2)}) copy-start(f32[128,2048]{1,0:T(8,128)} %convert_element_type.89) | copy-start | bytes 3145732
  70.9 5.3 %copy-start.7 = (f32[128,4]{1,0:T(8,128)S(1)}, f32[128,4]{1,0:T(8,128)}, u32[]{:S(2)}) copy-start(f32[128,4]{1,0:T(8,128)} %copy.40) | copy-start | bytes 6148
where the time goes:
time: 88.8 us; the launch traced here: 88.1 us
  local copies, waits for them, and re-layouts  27.1 us (31%)
  other arithmetic  18.1 us (20%)
  starting transfers between devices  18 us (20%)
  matrix products  8.18 us (9%)
  waiting for transfers between devices  7.67 us (9%)
  blocking collectives  7.33 us (8%)
  between operations  1.6 us (2%)
    reduce_sum x1, other arithmetic, body(): jnp.sum(cotangent.astype(jnp.float32)[:, None, :] * out_rows, axis=2)  11.4 us
    gather x2, local copies, waits for them, and re-layouts, body(): jnp.take(expert_out.reshape(-1, model_width), flat_index, axis=0)  8.83 us
    gather x2, local copies, waits for them, and re-layouts, body(): jnp.take(expert_grad.reshape(-1, model_width), flat_index, axis=0)  8.79 us
    all_to_all x1, waiting for transfers between devices, body(): lax.all_to_all(send_scaled, 'grp', split_axis=0, concat_axis=0, tiled=True)  7.41 us
    unnamed x1, blocking collectives  7.33 us
    all_to_all x1, starting transfers between devices, body(): lax.all_to_all(send_scaled, 'grp', split_axis=0, concat_axis=0, tiled=True)  4.26 us
    gather x5, local copies, waits for them, and re-layouts, body(): slot_index = jnp.take_along_axis(position, safe_ids, axis=1)  3.81 us
    all_to_all x1, starting transfers between devices, body(): lax.all_to_all(piece_out, 'grp', split_axis=0, concat_axis=0, tiled=True)  3.65 us
  transfers between devices with their start and end apart: 5, of which 2 were waited for; matrix products, arithmetic and copies ran while one was open for 37% of the time, Pallas kernels for 0%

commit v1 on v0

--- a/solution.py
+++ b/solution.py
@@ -2,9 +2,34 @@
 import jax.numpy as jnp
 from jax import lax
 from jax.sharding import PartitionSpec as P
+from jax.lax import axis_index, ppermute, psum
 
 PIECES = 4
 CAP = 32
+
+
+def touch_entries(inner_x):
+    which_axis = "grp"
+    built, outer = (psum(1, which_axis), axis_index(which_axis))
+    r2 = inner_x.shape[0] // built
+    w1 = list(inner_x.shape)
+    w1[0] = r2
+    lower = w1[0]
+    w1[0] = lower * built
+    extra = jnp.zeros(w1, inner_x.dtype)
+    no = 0
+    while no < built:
+        low = lax.dynamic_slice_in_dim(inner_x, (outer ^ no) * r2, r2, axis=0)
+        if no:
+            steps_seen = []
+            j = 0
+            while j < built:
+                steps_seen.append((j, j ^ no))
+                j += 1
+            low = ppermute(low, which_axis, steps_seen)
+        extra = lax.dynamic_update_slice_in_dim(extra, low, (outer ^ no) * lower, axis=0)
+        no += 1
+    return extra
 
 
 def joined(value, axis, combine):
@@ -138,7 +163,7 @@
         group_size, 2, half_cap, model_width
     )
     recv_rows = lax.all_to_all(send_rows, "grp", split_axis=0, concat_axis=0, tiled=True)
-    recv_scaled = lax.all_to_all(send_scaled, "grp", split_axis=0, concat_axis=0, tiled=True)
+    recv_scaled = touch_entries(send_scaled)
     item_count = recv_rows.shape[1]
     flat_rows = recv_rows.reshape(-1, model_width)
     flat_scaled = recv_scaled.reshape(-1, model_width)

time: 88.8 us -> 84.9 us (0.956)
  waiting for transfers between devices: 7.67 us -> 0.02 us
  local copies, waits for them, and re-layouts: 27.1 us -> 33.1 us
  starting transfers between devices: 18 us -> 15.6 us
    all_to_all x1 -> x0, waiting for transfers between devices: 7.41 us -> none  [body(): lax.all_to_all(send_scaled, 'grp', split_axis=0, concat_axis=0, tiled=True)]
    dynamic_update_slice x0 -> x4, local copies, waits for them, and re-layouts: none -> 5.37 us  [touch_entries(): lax.dynamic_update_slice_in_dim(extra, low, (outer ^ no) * lower, axis=0)]
    all_to_all x1 -> x0, starting transfers between devices: 4.26 us -> none  [body(): lax.all_to_all(send_scaled, 'grp', split_axis=0, concat_axis=0, tiled=True)]
    ppermute x0 -> x3, starting transfers between devices: none -> 3.15 us  [touch_entries(): low = ppermute(low, which_axis, steps_seen)]
    ppermute x1, starting transfers between devices: 3.05 us -> 1.77 us  [from_behind(): return lax.ppermute(value, axis, pairs)]
    dot_general x1, matrix products: 1.24 us -> 0.19 us  [body(): jnp.einsum('ect,td->ecd', select_bf, tokens, preferred_element_type=jnp.f...]
    dot_general x1, matrix products: 0.22 us -> 1.27 us  [body(): jnp.einsum('ect,td->ecd', select_bf, cotangent, preferred_element_type=jn...]
    unnamed x37 -> x41, local copies, waits for them, and re-layouts: 2.89 us -> 3.52 us
  transfers between devices with their start and end apart: 5 -> 7, of which waited for: 2 -> 0; matrix products, arithmetic and copies ran while one was open for 37% -> 42% of each run, Pallas kernels for 0% -> 0%
where the time goes in v1:
time: 84.9 us; the launch traced here: 84.2 us
  local copies, waits for them, and re-layouts  33.1 us (39%)
  other arithmetic  18.2 us (21%)
  starting transfers between devices  15.6 us (18%)
  matrix products  8.2 us (10%)
  blocking collectives  7.33 us (9%)
  between operations  1.61 us (2%)
    reduce_sum x1, other arithmetic, body(): jnp.sum(cotangent.astype(jnp.float32)[:, None, :] * out_rows, axis=2)  11.4 us
    gather x2, local copies, waits for them, and re-layouts, body(): jnp.take(expert_out.reshape(-1, model_width), flat_index, axis=0)  8.83 us
    gather x2, local copies, waits for them, and re-layouts, body(): jnp.take(expert_grad.reshape(-1, model_width), flat_index, axis=0)  8.79 us
    unnamed x1, blocking collectives  7.33 us
    dynamic_update_slice x4, local copies, waits for them, and re-layouts, touch_entries(): lax.dynamic_update_slice_in_dim(extra, low, (outer ^ no) * lower, axis=0)  5.37 us
    gather x5, local copies, waits for them, and re-layouts, body(): slot_index = jnp.take_along_axis(position, safe_ids, axis=1)  3.81 us
    all_to_all x1, starting transfers between devices, body(): lax.all_to_all(piece_out, 'grp', split_axis=0, concat_axis=0, tiled=True)  3.65 us
    all_to_all x1, starting transfers between devices, body(): lax.all_to_all(piece_grad, 'grp', split_axis=0, concat_axis=0, tiled=True)  3.6 us
  transfers between devices with their start and end apart: 7, of which 0 were waited for; matrix products, arithmetic and copies ran while one was open for 42% of the time, Pallas kernels for 0%

profile of v1, /device:TPU:0, one launch (start us, length us, event | category | flops | bytes accessed | tf_op | source)
XLA Modules:
  0.0 84.2 jit_solution(3172505145111833586)
XLA Ops:
  0.7 0.8 select_reduce_fusion
  1.6 0.2 reduce_window_sum.13
  1.9 0.1 convolution_bitcast_fusion
  2.0 1.3 %fusion.17 = bf16[32,2048]{1,0:T(8,128)(2,1)S(1)} fusion(bf16[128,2048]{1,0:T(8,128)(2,1)} %param.15, f32[32]{0:T(128)S(1)} %convolution_bitcast_fusion, s32[128]{0:T(128)S(1)} %sub.111, pred[128]{0:T(512)(128)(4,1)S(1)} %broadcast_compare_fusion.2), kind=kOutput, calls=%fused_computation.35 | convolution fusion | flops 16916480 | bytes 656128 | tf_op jit(solution)/shard_map/ect,td->ecd/dot_general | solution.py:159
  3.3 0.6 collective-permute-start
  3.9 2.6 %collective-permute-start.1 = (bf16[1,2,16,2048]{3,2,1,0:T(8,128)(2,1)S(1)}, bf16[1,2,16,2048]{3,2,1,0:T(8,128)(2,1)}, u32[]{:S(2)}, u32[]{:S(2)}) collective-permute-start(bf16[1,2,16,2048]{3,2,1,0:T(8,128)(2,1)S(1)} %bitcast.131), channel_id=1, source_target_pairs={{0,2},{1,3},{2,0},{3,1},{4,6},{5,7},{6,4},{7,5},{8,10},{9,11},{10,... | collective-permute-start | bytes 393224 | tf_op jit(solution)/shard_map/ppermute | solution.py:29
  6.5 1.8 %collective-permute-start.3 = (bf16[1,8,37984]{2,1,0:T(8,128)(2,1)}, bf16[1,8,37984]{2,1,0:T(8,128)(2,1)S(1)}, u32[]{:S(2)}, u32[]{:S(2)}) collective-permute-start(bf16[1,8,37984]{2,1,0:T(8,128)(2,1)} %param.22), channel_id=1, source_target_pairs={{0,4},{4,8},{8,12},{12,16},{16,20},{20,24},{24,28},{28,0},{1,5},{5... | collective-permute-start | bytes 1823240 | tf_op jit(solution)/shard_map/ppermute | solution.py:48
  8.2 0.2 convolution_convert_fusion.1
  8.4 0.9 %broadcast_in_dim.64 = bf16[4,2,16,2048]{3,2,1,0:T(8,128)(2,1)} broadcast(bf16[2,16,2048]{2,1,0:T(8,128)(2,1)S(1)} %bitcast.129), dimensions={1,2,3} | broadcast | bytes 655360 | tf_op jit(solution)/shard_map/broadcast_in_dim | solution.py:161
  9.3 3.5 %all-to-all-start = ((bf16[4,2,16,2048]{3,2,1,0:T(8,128)(2,1)}), bf16[4,2,16,2048]{3,2,1,0:T(8,128)(2,1)S(1)}, u32[]{:S(2)}, u32[]{:S(2)}) async-start(bf16[4,2,16,2048]{3,2,1,0:T(8,128)(2,1)} %broadcast_in_dim.64), calls=%async_computation | async-start | bytes 1048576 | tf_op jit(solution)/shard_map/all_to_all | solution.py:165
  12.8 0.1 copy.44
  13.1 3.4 %gather_fusion = s32[512]{0:T(512)S(1)} fusion(s32[128,1]{1,0:T(8,128)S(1)} %get-tuple-element.386, s32[512]{0:T(512)S(1)} %reshape.293), kind=kCustom, calls=%fused_computation.2 | custom fusion | bytes 8192 | tf_op jit(solution)/shard_map/jit(take_along_axis)/gather | solution.py:185
  16.7 0.4 reduce_max.36
  17.2 0.6 dynamic-slice.4
  18.4 0.8 %broadcast_in_dim.67 = bf16[4,2,16,2048]{3,2,1,0:T(8,128)(2,1)} broadcast(bf16[]{:T(256)} %constant.86.clone.1), dimensions={} | broadcast | bytes 524290 | tf_op jit(solution)/shard_map/broadcast_in_dim | solution.py:19
  19.3 0.7 constant_dynamic-update-slice_fusion.3
  20.0 1.2 %convert_element_type.89 = f32[128,2048]{1,0:T(8,128)} convert(bf16[128,2048]{1,0:T(8,128)(2,1)S(1)} %copy-done.5) | non-fusion elementwise | flops 262144 | bytes 1572864 | tf_op jit(solution)/shard_map/convert_element_type | solution.py:198
  21.2 0.7 copy.40
  22.1 0.1 copy.41
  22.3 0.1 copy.46
  22.5 1.6 %constant_dynamic-update-slice_fusion.2 = bf16[4,2,16,2048]{3,2,1,0:T(8,128)(2,1)} fusion(bf16[4,2,16,2048]{3,2,1,0:T(8,128)(2,1)} %constant_dynamic-update-slice_fusion.3, bf16[1,2,16,2048]{3,2,1,0:T(8,128)(2,1)} %collective-permute-done, s32[]{:T(128)S(6)} %select_n.66), kind=kLoop, calls=%fused_computation.97 | loop fusion | bytes 262148 | tf_op jit(solution)/shard_map/dynamic_update_slice | solution.py:30
  24.0 1.6 %constant_dynamic-update-slice_fusion.1 = bf16[4,2,16,2048]{3,2,1,0:T(8,128)(2,1)} fusion(bf16[4,2,16,2048]{3,2,1,0:T(8,128)(2,1)} %constant_dynamic-update-slice_fusion.2, bf16[1,2,16,2048]{3,2,1,0:T(8,128)(2,1)} %collective-permute-done.1, s32[]{:T(128)S(6)} %select_n.67), kind=kLoop, calls=%fused_computation.96 | loop fusion | bytes 262148 | tf_op jit(solution)/shard_map/dynamic_update_slice | solution.py:30
  25.6 1.6 %constant_dynamic-update-slice_fusion = bf16[4,2,16,2048]{3,2,1,0:T(8,128)(2,1)} fusion(bf16[4,2,16,2048]{3,2,1,0:T(8,128)(2,1)} %constant_dynamic-update-slice_fusion.1, bf16[1,2,16,2048]{3,2,1,0:T(8,128)(2,1)} %collective-permute-done.2, s32[]{:T(128)S(6)} %select_n.68), kind=kLoop, calls=%fused_computation.95 | loop fusion | bytes 262148 | tf_op jit(solution)/shard_map/dynamic_update_slice | solution.py:30
  27.2 2.3 %fusion.35 = f32[128,176]{0,1:T(8,128)} fusion(bf16[128,2048]{1,0:T(8,128)(2,1)} %bitcast.18, bf16[1,176,2048]{2,1,0:T(8,128)(2,1)} %param.20), kind=kOutput, calls=%fused_computation.61 | convolution fusion | flops 92274688 | bytes 1335296 | tf_op jit(solution)/shard_map/dot_general | solution.py:70
  29.5 0.4 fusion.43
  29.9 0.4 fusion.39
  30.3 0.6 copy-done.7
  31.0 0.4 fusion.41
  31.3 1.1 %fusion.16 = bf16[128,2048]{1,0:T(8,128)(2,1)} fusion(f32[128,2048]{1,0:T(8,128)S(1)} %fusion.41, bf16[1,2048,176]{1,2,0:T(8,128)(2,1)S(1)} %copy-done.3, f32[128,176]{0,1:T(8,128)S(1)} %copy-done.6, f32[128,176]{0,1:T(8,128)S(1)} %fusion.43), kind=kOutput, calls=%fused_computation.32 | convolution fusion | flops 92934144 | bytes 2473984 | tf_op jit(solution)/shard_map/dot_general | solution.py:79
  32.5 3.6 %all-to-all-start.2 = ((bf16[4,2,16,2048]{3,2,1,0:T(8,128)(2,1)}), bf16[4,2,16,2048]{3,2,1,0:T(8,128)(2,1)S(1)}, u32[]{:S(2)}, u32[]{:S(2)}) async-start(bf16[4,2,16,2048]{3,2,1,0:T(8,128)(2,1)} %bitcast.19), calls=%async_computation.2 | async-start | bytes 1048576 | tf_op jit(solution)/shard_map/all_to_all | solution.py:175
  36.1 2.0 %convolution_convert_fusion = bf16[128,2048]{1,0:T(8,128)(2,1)} fusion(bf16[1,176,2048]{2,1,0:T(8,128)(2,1)S(1)} %copy-done.4, f32[128,176]{0,1:T(8,128)} %copy-done.7, f32[128,176]{0,1:T(8,128)S(1)} %fusion.43), kind=kOutput, calls=%fused_computation.33 | convolution fusion | flops 92672000 | bytes 1425408 | tf_op jit(solution)/shard_map/dot_general | solution.py:64
  38.1 0.4 reduce_max.40
  38.7 1.2 %fusion.33 = (f32[8]{0:T(128)S(1)}, f32[8]{0:T(128)S(1)}, f32[8]{0:T(128)S(1)}, f32[8]{0:T(128)S(1)}) fusion(bf16[1,8,37984]{2,1,0:T(8,128)(2,1)S(1)} %collective-permute-done.3, bf16[1,8,37984]{2,1,0:T(8,128)(2,1)S(1)} %copy-done.1, f32[8]{0:T(128)S(1)} %reduce_max.45, s32[8]{0:T(128)S(1)} %bitcast.140, s32[37984]{0:T(1024)S(1)} %iota_add_fusion, ...), kind=kLoop, calls=%fused_computation.56 | loop fusion | flops 3646432 | bytes 1367648 | tf_op jit(solution)/shard_map/reduce_sum | solution.py:112
  39.8 0.2 dynamic-update-slice.1
  40.1 0.2 dynamic-update-slice.3
  40.3 0.2 dynamic-update-slice.4
  40.5 0.2 dynamic-update-slice.5
  40.7 7.3 %all-reduce.6 = (f32[32]{0:T(128)S(1)}, f32[32]{0:T(128)S(1)}, f32[32]{0:T(128)S(1)}, f32[32]{0:T(128)S(1)}, f32[32]{0:T(128)S(1)}, /*index=5*/f32[32]{0:T(128)S(1)}) all-reduce(f32[32]{0:T(128)S(1)} %convert_dynamic-update-slice_fusion.1, f32[32]{0:T(128)S(1)} %dynamic-update-slice.1, ...), channel_id=2, replica_groups=mesh['peer'=8,'grp'=4] {'grp'}, use_global_device_ids=true, to_apply=%add | all-reduce | flops 192 | bytes 1536
  48.5 0.3 while.25
  48.8 0.5 subtract_bitcast_fusion
  49.3 3.7 %all-to-all-start.1 = ((bf16[4,2,16,2048]{3,2,1,0:T(8,128)(2,1)}), bf16[4,2,16,2048]{3,2,1,0:T(8,128)(2,1)S(1)}, u32[]{:S(2)}, u32[]{:S(2)}) async-start(bf16[4,2,16,2048]{3,2,1,0:T(8,128)(2,1)} %bitcast.128), calls=%async_computation.1 | async-start | bytes 1048576 | tf_op jit(solution)/shard_map/all_to_all | solution.py:174
  53.0 1.4 %fusion.29 = bf16[1,8,37984]{2,1,0:T(8,128)(2,1)} fusion(bf16[1,8,37984]{2,1,0:T(8,128)(2,1)S(1)} %copy-done.1, bf16[1,8,37984]{2,1,0:T(8,128)(2,1)S(1)} %collective-permute-done.3, f32[8]{0:T(128)S(1)} %get-tuple-element.380, s32[37984]{0:T(1024)S(1)} %iota_add_fusion, f32[8]{0:T(128)S(1)} %get-tuple-element.379, s32[8]{0:T(128)S(1)} %bitcast.141), kind=kLoop, calls=%fused_computation.52 | loop fusion | flops 3038720 | bytes 1975264 | tf_op jit(solution)/shard_map/convert_element_type | solution.py:124
  54.5 3.6 %gather_fusion.2 = f32[512,2048]{1,0:T(8,128)} fusion(f32[32,2048]{1,0:T(8,128)S(1)} %bitcast.125, s32[1024]{0:T(1024)S(1)} %pad_clamp_fusion), kind=kCustom, calls=%fused_computation.1.clone | custom fusion | bytes 8390656 | tf_op jit(solution)/shard_map/jit(_take)/gather | solution.py:194
  58.1 5.2 %reshape.363 = f32[128,4,2048]{2,1,0:T(4,128)} reshape(f32[512,2048]{1,0:T(8,128)} %gather_fusion.2) | data formatting | bytes 8388608 | tf_op jit(solution)/shard_map/jit(_take)/gather | solution.py:194
  63.4 3.6 %gather_fusion.1 = f32[512,2048]{1,0:T(8,128)} fusion(f32[32,2048]{1,0:T(8,128)S(1)} %bitcast.124, s32[1024]{0:T(1024)S(1)} %pad_clamp_fusion), kind=kCustom, calls=%fused_computation.clone | custom fusion | bytes 8390656 | tf_op jit(solution)/shard_map/jit(_take)/gather | solution.py:189
  67.0 5.3 %reshape.359 = f32[128,4,2048]{2,1,0:T(4,128)} reshape(f32[512,2048]{1,0:T(8,128)} %gather_fusion.1) | data formatting | bytes 8388608 | tf_op jit(solution)/shard_map/jit(_take)/gather | solution.py:189
  72.2 11.4 %multiply_reduce_fusion = (f32[128,4]{1,0:T(8,128)S(1)}, bf16[128,2048]{1,0:T(8,128)(2,1)}, bf16[128,2048]{1,0:T(8,128)(2,1)}) fusion(f32[128,4,2048]{2,1,0:T(4,128)} %reshape.359, f32[128,2048]{1,0:T(8,128)S(1)} %copy-done.2, pred[128,4]{1,0:T(8,128)(4,1)S(1)} %copy.46, pred[128,4]{1,0:T(8,128)(4,1)S(1)} %copy.41, f32[128,4]{1,0:T(8,128)S(1)} %copy-done.9, ...), kind=kLoop, calls=%fused_computation.29 | loop fusion | flops 8912384 | bytes 10490880 | tf_op jit(solution)/shard_map/reduce_sum | solution.py:198
  83.6 0.7 copy.50
  (79 shorter events, 2.0 us)
Async XLA Ops:
  0.6 28.9 %copy-start = (bf16[1,2048,176]{1,2,0:T(8,128)(2,1)S(1)}, bf16[1,2048,176]{1,2,0:T(8,128)(2,1)}, u32[]{:S(2)}) copy-start(bf16[1,2048,176]{1,2,0:T(8,128)(2,1)} %param.18) | copy-start | bytes 2162692
  0.6 7.6 %copy-start.8 = (bf16[128,2048]{1,0:T(8,128)(2,1)S(1)}, bf16[128,2048]{1,0:T(8,128)(2,1)}, u32[]{:S(2)}) copy-start(bf16[128,2048]{1,0:T(8,128)(2,1)} %param.14) | copy-start | bytes 1572868
  3.3 9.5 %copy-start.10 = (s32[128,4]{0,1:T(4,128)S(1)}, s32[128,4]{0,1:T(4,128)}, u32[]{:S(2)}) copy-start(s32[128,4]{0,1:T(4,128)} %param.16) | copy-start | bytes 6148
  3.3 19.1 %collective-permute-start = (bf16[1,2,16,2048]{3,2,1,0:T(8,128)(2,1)S(1)}, bf16[1,2,16,2048]{3,2,1,0:T(8,128)(2,1)}, u32[]{:S(2)}, u32[]{:S(2)}) collective-permute-start(bf16[1,2,16,2048]{3,2,1,0:T(8,128)(2,1)S(1)} %bitcast.130), channel_id=1, source_target_pairs={{0,1},{1,0},{2,3},{3,2},{4,5},{5,4},{6,7},{7,6},{8,9},{9,8},{10,11... | collective-permute-start | bytes 393224 | tf_op jit(solution)/shard_map/ppermute | solution.py:29
  3.9 20.2 %collective-permute-start.1 = (bf16[1,2,16,2048]{3,2,1,0:T(8,128)(2,1)S(1)}, bf16[1,2,16,2048]{3,2,1,0:T(8,128)(2,1)}, u32[]{:S(2)}, u32[]{:S(2)}) collective-permute-start(bf16[1,2,16,2048]{3,2,1,0:T(8,128)(2,1)S(1)} %bitcast.131), channel_id=1, source_target_pairs={{0,2},{1,3},{2,0},{3,1},{4,6},{5,7},{6,4},{7,5},{8,10},{9,11},{10,... | collective-permute-start | bytes 393224 | tf_op jit(solution)/shard_map/ppermute | solution.py:29
  6.4 19.2 %collective-permute-start.2 = (bf16[1,2,16,2048]{3,2,1,0:T(8,128)(2,1)S(1)}, bf16[1,2,16,2048]{3,2,1,0:T(8,128)(2,1)}, u32[]{:S(2)}, u32[]{:S(2)}) collective-permute-start(bf16[1,2,16,2048]{3,2,1,0:T(8,128)(2,1)S(1)} %bitcast.132), channel_id=1, source_target_pairs={{0,3},{1,2},{2,1},{3,0},{4,7},{5,6},{6,5},{7,4},{8,11},{9,10},{10,... | collective-permute-start | bytes 393224 | tf_op jit(solution)/shard_map/ppermute | solution.py:29
  6.5 31.7 %collective-permute-start.3 = (bf16[1,8,37984]{2,1,0:T(8,128)(2,1)}, bf16[1,8,37984]{2,1,0:T(8,128)(2,1)S(1)}, u32[]{:S(2)}, u32[]{:S(2)}) collective-permute-start(bf16[1,8,37984]{2,1,0:T(8,128)(2,1)} %param.22), channel_id=1, source_target_pairs={{0,4},{4,8},{8,12},{12,16},{16,20},{20,24},{24,28},{28,0},{1,5},{5... | collective-permute-start | bytes 1823240 | tf_op jit(solution)/shard_map/ppermute | solution.py:48
  9.3 20.2 %all-to-all-start = ((bf16[4,2,16,2048]{3,2,1,0:T(8,128)(2,1)}), bf16[4,2,16,2048]{3,2,1,0:T(8,128)(2,1)S(1)}, u32[]{:S(2)}, u32[]{:S(2)}) async-start(bf16[4,2,16,2048]{3,2,1,0:T(8,128)(2,1)} %broadcast_in_dim.64), calls=%async_computation | async-start | bytes 1048576 | tf_op jit(solution)/shard_map/all_to_all | solution.py:165
  13.1 3.7 %copy-start.1 = (bf16[1,8,37984]{2,1,0:T(8,128)(2,1)S(1)}, bf16[1,8,37984]{2,1,0:T(8,128)(2,1)}, u32[]{:S(2)}) copy-start(bf16[1,8,37984]{2,1,0:T(8,128)(2,1)} %param.21) | copy-start | bytes 1823236
  13.1 4.1 %copy-start.13 = (u32[32]{0:T(128)S(1)}, u32[32]{0:T(128)}, u32[]{:S(2)}) copy-start(u32[32]{0:T(128)} %constant.115) | copy-start | bytes 388
  16.5 3.5 %copy-start.5 = (bf16[128,2048]{1,0:T(8,128)(2,1)S(1)}, bf16[128,2048]{1,0:T(8,128)(2,1)}, u32[]{:S(2)}) copy-start(bf16[128,2048]{1,0:T(8,128)(2,1)} %param.15) | copy-start | bytes 1572868
  17.2 4.0 %copy-start.11 = (f32[128,4]{0,1:T(4,128)S(1)}, f32[128,4]{0,1:T(4,128)}, u32[]{:S(2)}) copy-start(f32[128,4]{0,1:T(4,128)} %param.17) | copy-start | bytes 6148
  27.2 2.7 %copy-start.3 = (bf16[1,2048,176]{1,2,0:T(8,128)(2,1)S(1)}, bf16[1,2048,176]{1,2,0:T(8,128)(2,1)}, u32[]{:S(2)}) copy-start(bf16[1,2048,176]{1,2,0:T(8,128)(2,1)} %param.19) | copy-start | bytes 2162692
  29.5 1.4 %copy-start.6 = (f32[128,176]{0,1:T(8,128)S(1)}, f32[128,176]{0,1:T(8,128)}, u32[]{:S(2)}) copy-start(f32[128,176]{0,1:T(8,128)} %fusion.35) | copy-start | bytes 270340
  30.3 0.6 copy-start.7
  32.5 3.6 %copy-start.4 = (bf16[1,176,2048]{2,1,0:T(8,128)(2,1)S(1)}, bf16[1,176,2048]{2,1,0:T(8,128)(2,1)}, u32[]{:S(2)}) copy-start(bf16[1,176,2048]{2,1,0:T(8,128)(2,1)} %param.20) | copy-start | bytes 2162692
  32.5 16.9 %all-to-all-start.2 = ((bf16[4,2,16,2048]{3,2,1,0:T(8,128)(2,1)}), bf16[4,2,16,2048]{3,2,1,0:T(8,128)(2,1)S(1)}, u32[]{:S(2)}, u32[]{:S(2)}) async-start(bf16[4,2,16,2048]{3,2,1,0:T(8,128)(2,1)} %bitcast.19), calls=%async_computation.2 | async-start | bytes 1048576 | tf_op jit(solution)/shard_map/all_to_all | solution.py:175
  36.1 2.6 %copy-start.12 = (s32[1,8]{1,0:T(1,128)S(1)}, s32[1,8]{1,0:T(1,128)}, u32[]{:S(2)}) copy-start(s32[1,8]{1,0:T(1,128)} %param.23) | copy-start | bytes 100
  49.3 14.0 %all-to-all-start.1 = ((bf16[4,2,16,2048]{3,2,1,0:T(8,128)(2,1)}), bf16[4,2,16,2048]{3,2,1,0:T(8,128)(2,1)S(1)}, u32[]{:S(2)}, u32[]{:S(2)}) async-start(bf16[4,2,16,2048]{3,2,1,0:T(8,128)(2,1)} %bitcast.128), calls=%async_computation.1 | async-start | bytes 1048576 | tf_op jit(solution)/shard_map/all_to_all | solution.py:174
  67.0 5.3 %copy-start.2 = (f32[128,2048]{1,0:T(8,128)S(1)}, f32[128,2048]{1,0:T(8,128)}, u32[]{:S(2)}) copy-start(f32[128,2048]{1,0:T(8,128)} %convert_element_type.89) | copy-start | bytes 3145732
  67.0 5.3 %copy-start.9 = (f32[128,4]{1,0:T(8,128)S(1)}, f32[128,4]{1,0:T(8,128)}, u32[]{:S(2)}) copy-start(f32[128,4]{1,0:T(8,128)} %copy.40) | copy-start | bytes 6148
